TPU v7x, 512 devices: a whole 4x8x8 slice. The times are simulated.
512 devices in a mesh: grp: 16 (over z, y_lo), col: 32 (over x, y_hi, core).
Axes of the slice: x: 4, y: 8 (y_hi: 4, y_lo: 2; y = y_hi * 2 + y_lo), z: 8, core: 2. Of those that a mesh axis runs over, the one named last changes fastest.
Arguments:
- descriptors: bfloat16 [10, 32, 128, 4096], P(None, None, 'grp', 'col'), may hold values from -6 to 6
- solid_temp: float32 [32, 128, 4096], P(None, 'grp', 'col'), may hold values from -6 to 6
- fluid_temp: float32 [32, 128, 4096], P(None, 'grp', 'col'), may hold values from -6 to 6
- material: int32 [32, 128, 4096], P(None, 'grp', 'col'), may hold values from 0 to 3
- fixed_mask: int32 [32, 128, 4096], P(None, 'grp', 'col'), may hold values 0 or 1
- solid_cond: float32 [4], replicated, may hold values from 0.3 to 1.5
- fluid_cond: float32 [4], replicated, may hold values from 0.3 to 1.5
- w_in: bfloat16 [12, 64], replicated, may hold values from -1.75 to 1.75
- b_in: float32 [64], replicated, may hold values from -3 to 3
- w_mid: bfloat16 [64, 64], replicated, may hold values from -0.75 to 0.75
- b_mid: float32 [64], replicated, may hold values from -3 to 3
- w_out: bfloat16 [64, 2], replicated, may hold values from -0.75 to 0.75
- b_out: float32 [2], replicated, may hold values from -3 to 3
- solid_cot: float32 [32, 128, 4096], P(None, 'grp', 'col'), may hold values from -18 to 18
- fluid_cot: float32 [32, 128, 4096], P(None, 'grp', 'col'), may hold values from -18 to 18
Outputs:
- adj_solid: float32 [32, 128, 4096], P(None, 'grp', 'col')
- adj_fluid: float32 [32, 128, 4096], P(None, 'grp', 'col')
- grad_w_in: float32 [12, 64], replicated
- grad_b_in: float32 [64], replicated
- grad_w_mid: float32 [64, 64], replicated
- grad_b_mid: float32 [64], replicated
- grad_w_out: float32 [64, 2], replicated
- grad_b_out: float32 [2], replicated
All inputs are finite; a program needn't handle non-finite values. No bound on the sum of `fixed_mask` on one device may be relied on, other than what follows from the above.
Results may differ from a plain program's by a relative error of at most 0.01.
The roundings to bfloat16 on the way count: a program that leaves them out, or rounds other values in their place, can miss the bound.
Values sent between devices are 32-bit elements; how exact they have to be, the bound alone decides.
No kernel may reach another device: no remote copies, remote signals or barrier semaphores. Data moves between devices by JAX's collectives and lax.ppermute only.
A program may use at most 64 MiB of HBM per device.

v0:
```python
import math
import jax
import jax.numpy as jnp
from jax import lax
from jax.sharding import PartitionSpec as P

time_step = 0.15
loss_gain = 16.0


def padded_2(block, sides, width):
    for axis, dim in sides:
        count = lax.axis_size(axis)
        forward = [(i, i + 1) for i in range(count - 1)]
        backward = [(target, source) for source, target in forward]
        low = lax.ppermute(
            lax.slice_in_dim(block, block.shape[dim] - width, None, axis=dim), axis, forward
        )
        high = lax.ppermute(lax.slice_in_dim(block, 0, width, axis=dim), axis, backward)
        block = jnp.concatenate([low, block, high], axis=dim)
    return block


def material_lookup(material, lookup_table):
    summed = jnp.zeros(material.shape, jnp.float32)
    for material_kind in range(lookup_table.shape[0]):
        summed = summed + jnp.where(material == material_kind, lookup_table[material_kind], 0.0)
    return summed


def neighbour_sum(padded, values_field):
    return (
        padded[:, :, 2:, 1:-1]
        + padded[:, :, :-2, 1:-1]
        + padded[:, :, 1:-1, 2:]
        + padded[:, :, 1:-1, :-2]
        - 4.0 * values_field
    )


def network(features, w_in, b_in, w_mid, b_mid, w_out, b_out):
    hidden_one = jnp.tanh(
        jnp.dot(w_in.T, features, preferred_element_type=jnp.float32) + b_in[:, None]
    ).astype(jnp.bfloat16)
    hidden_two = jnp.tanh(
        jnp.dot(w_mid.T, hidden_one, preferred_element_type=jnp.float32) + b_mid[:, None]
    ).astype(jnp.bfloat16)
    logits = jnp.dot(w_out.T, hidden_two, preferred_element_type=jnp.float32) + b_out[:, None]
    return (hidden_one, hidden_two, logits)


def coupling_terms(logits):
    transfer_coef = jax.nn.softplus(logits[0])
    area_coef = jax.nn.softplus(logits[1])
    return (transfer_coef * area_coef, transfer_coef, area_coef)


def backprop(features, hidden_one, hidden_two, logits, d_coupling, w_in, w_mid, w_out):
    coupling, transfer_coef, area_coef = coupling_terms(logits)
    d_logits = jnp.stack(
        [
            d_coupling * area_coef * jax.nn.sigmoid(logits[0]),
            d_coupling * transfer_coef * jax.nn.sigmoid(logits[1]),
        ]
    ).astype(jnp.bfloat16)
    d_hidden_two = (
        jnp.dot(w_out, d_logits, preferred_element_type=jnp.float32)
        * (1.0 - jnp.square(hidden_two.astype(jnp.float32)))
    ).astype(jnp.bfloat16)
    d_hidden_one = (
        jnp.dot(w_mid, d_hidden_two, preferred_element_type=jnp.float32)
        * (1.0 - jnp.square(hidden_one.astype(jnp.float32)))
    ).astype(jnp.bfloat16)
    d_features = jnp.dot(
        w_in[w_in.shape[0] - 2 :], d_hidden_one, preferred_element_type=jnp.float32
    )
    gradients = (
        jnp.dot(features, d_hidden_one.T, preferred_element_type=jnp.float32),
        jnp.sum(d_hidden_one.astype(jnp.float32), axis=1),
        jnp.dot(hidden_one, d_hidden_two.T, preferred_element_type=jnp.float32),
        jnp.sum(d_hidden_two.astype(jnp.float32), axis=1),
        jnp.dot(hidden_two, d_logits.T, preferred_element_type=jnp.float32),
        jnp.sum(d_logits.astype(jnp.float32), axis=1),
    )
    return (coupling, d_features, gradients)


def build_features(desc_line, solid_line, fluid_line):
    cells = solid_line.size
    return jnp.concatenate(
        [
            desc_line.reshape(desc_line.shape[0], cells),
            solid_line.reshape(1, cells).astype(jnp.bfloat16),
            fluid_line.reshape(1, cells).astype(jnp.bfloat16),
        ],
        axis=0,
    )


def forward_coupling(descriptors, solid, fluid, weights):

    def forward_one_line(line_index):
        desc_line = lax.dynamic_index_in_dim(descriptors, line_index, 1, keepdims=False)
        solid_line = lax.dynamic_index_in_dim(solid, line_index, 0, keepdims=False)
        fluid_line = lax.dynamic_index_in_dim(fluid, line_index, 0, keepdims=False)
        features = build_features(desc_line, solid_line, fluid_line)
        logits = network(features, *weights)[2]
        return coupling_terms(logits)[0].reshape(solid_line.shape)

    return lax.map(forward_one_line, jnp.arange(solid.shape[0], dtype=jnp.int32))


def backward_lines(descriptors, solid, fluid, d_coupling, weights, running):
    w_in, b_in, w_mid, b_mid, w_out, b_out = weights

    def backward_one_line(running, line_index):
        desc_line = lax.dynamic_index_in_dim(descriptors, line_index, 1, keepdims=False)
        solid_line = lax.dynamic_index_in_dim(solid, line_index, 0, keepdims=False)
        fluid_line = lax.dynamic_index_in_dim(fluid, line_index, 0, keepdims=False)
        d_line = lax.dynamic_index_in_dim(d_coupling, line_index, 0, keepdims=False)
        features = build_features(desc_line, solid_line, fluid_line)
        hidden_one, hidden_two, logits = network(features, *weights)
        coupling, d_features, gradients = backprop(
            features, hidden_one, hidden_two, logits, d_line.reshape(-1), w_in, w_mid, w_out
        )
        running = tuple((left + right for left, right in zip(running, gradients)))
        line_shape = solid_line.shape
        return (running, (coupling.reshape(line_shape), d_features.reshape((2,) + line_shape)))

    running, (coupling, d_features) = lax.scan(
        backward_one_line, running, jnp.arange(solid.shape[0], dtype=jnp.int32)
    )
    return (running, coupling, jnp.moveaxis(d_features, 1, 0))


def advance(state, state_padded, conduct, free_cell, first_coupling):
    coupled = first_coupling * (state[1] - state[0])
    return state + time_step * free_cell * (
        conduct * neighbour_sum(state_padded, state) + jnp.stack([coupled, -coupled])
    )


def shards(
    descriptors,
    solid_temp,
    fluid_temp,
    material,
    fixed_mask,
    solid_cond,
    fluid_cond,
    w_in,
    b_in,
    w_mid,
    b_mid,
    w_out,
    b_out,
    solid_cot,
    fluid_cot,
):
    weights = (w_in, b_in, w_mid, b_mid, w_out, b_out)
    conduct = jnp.stack(
        [material_lookup(material, solid_cond), material_lookup(material, fluid_cond)]
    )
    free_cell = 1.0 - fixed_mask.astype(jnp.float32)
    state = jnp.stack([solid_temp, fluid_temp])
    first_coupling = forward_coupling(descriptors, state[0], state[1], weights)
    cotangent = jnp.stack([solid_cot, fluid_cot])
    upstream = time_step * free_cell * cotangent
    pushed = conduct * upstream
    state_padded = padded_2(state, (("grp", 2), ("col", 3)), 1)
    later = advance(state, state_padded, conduct, free_cell, first_coupling)
    pushed_rim = padded_2(pushed, (("grp", 2), ("col", 3)), 1)
    running = (
        jnp.zeros(w_in.shape, jnp.float32),
        jnp.zeros(b_in.shape, jnp.float32),
        jnp.zeros(w_mid.shape, jnp.float32),
        jnp.zeros(b_mid.shape, jnp.float32),
        jnp.zeros(w_out.shape, jnp.float32),
        jnp.zeros(b_out.shape, jnp.float32),
    )
    d_coupling = (later[1] - later[0]) * (upstream[0] - upstream[1])
    running, coupling, d_features = backward_lines(
        descriptors, later[0], later[1], d_coupling, weights, running
    )
    swing_term = coupling * (upstream[1] - upstream[0])
    cotangent = (
        cotangent
        + neighbour_sum(pushed_rim, pushed)
        + jnp.stack([swing_term, -swing_term])
        + d_features
    )
    upstream = time_step * free_cell * cotangent
    pushed = conduct * upstream
    pushed_rim = padded_2(pushed, (("grp", 2), ("col", 3)), 1)
    d_coupling = (state[1] - state[0]) * (upstream[0] - upstream[1])
    running, coupling, d_features = backward_lines(
        descriptors, state[0], state[1], d_coupling, weights, running
    )
    swing_term = coupling * (upstream[1] - upstream[0])
    cotangent = (
        cotangent
        + neighbour_sum(pushed_rim, pushed)
        + jnp.stack([swing_term, -swing_term])
        + d_features
    )
    summed = lax.psum(
        (running[0], running[1], running[2], running[3], running[4], running[5]), ("grp", "col")
    )
    cell_count = solid_temp.size * lax.axis_size("grp") * lax.axis_size("col")
    scale = loss_gain / math.sqrt(cell_count)
    return (
        cotangent[0],
        cotangent[1],
        summed[0] * scale,
        summed[1] * scale,
        summed[2] * scale,
        summed[3] * scale,
        summed[4] * scale,
        summed[5] * scale,
    )


def solution(mesh):
    placed = (
        P(None, None, "grp", "col"),
        P(None, "grp", "col"),
        P(None, "grp", "col"),
        P(None, "grp", "col"),
        P(None, "grp", "col"),
        P(),
        P(),
        P(),
        P(),
        P(),
        P(),
        P(),
        P(),
        P(None, "grp", "col"),
        P(None, "grp", "col"),
    )
    return jax.shard_map(
        shards,
        mesh=mesh,
        in_specs=placed,
        out_specs=(P(None, "grp", "col"), P(None, "grp", "col"), P(), P(), P(), P(), P(), P()),
        check_vma=False,
    )
```

profile of v0, /device:TPU:19, one launch (start us, length us, event | category | flops | bytes accessed | tf_op | source)
XLA Modules:
  0.0 927.6 jit_solution(6519059867842374332)
XLA Ops:
  0.7 1.2 fusion.89
  1.9 1.3 collective-permute-start.4
  3.2 4.0 collective-permute-start.5
  8.4 2.7 add_bitcast_fusion.1
  11.1 2.7 add_bitcast_fusion
  14.0 1.3 collective-permute-start
  15.3 4.7 collective-permute-start.1
  20.8 128.7 %while.59 = (s32[]{:T(128)}, f32[32,8,128]{2,1,0:T(8,128)S(1)}, s32[32]{0:T(128)S(1)}, bf16[10,32,8,128]{3,2,1,0:T(8,128)(2,1)}, bf16[32,8,128]{2,1,0:T(8,128)(2...) while((s32[]{:T(128)}, f32[32,8,128]{2,1,0:T(8,128)S(1)}, ...), condition=%wide.region_1.2_spmd, body=%wide.region_0.1_spmd.sunk | while | flops 10574853 | bytes 510433 | solution.py:110
  150.6 6.4 collective-permute-start.7
  157.0 1.9 collective-permute-start.6
  159.6 1.2 fusion.96
  160.7 5.7 collective-permute-start.3
  166.5 1.9 collective-permute-start.2
  168.4 2.3 collective-permute-done.7
  170.7 1.9 collective-permute-done.6
  173.7 415.8 %while.61 = (s32[]{:T(128)}, f32[12,64]{1,0:T(8,128)S(1)}, f32[64]{0:T(128)}, f32[64,64]{1,0:T(8,128)S(1)}, f32[64]{0:T(128)}, /*index=5*/f32[64,2]{0,1:T(2,128)...) while((s32[]{:T(128)}, f32[12,64]{1,0:T(8,128)S(1)}, ...), condition=%wide.region_6.7_spmd.clone, body=%wide.region_2.6_spmd.clone.sunk | while | flops 30749576 | bytes 3280900 | solution.py:130
  193.1 0.9 convert_reduce_fusion.16
  232.0 0.9 convert_reduce_fusion.16
  245.0 0.9 convert_reduce_fusion.16
  258.0 0.9 convert_reduce_fusion.16
  297.0 0.9 convert_reduce_fusion.16
  310.0 0.9 convert_reduce_fusion.16
  323.0 0.9 convert_reduce_fusion.16
  569.9 0.9 convert_reduce_fusion.16
  591.3 1.3 collective-permute-start.8
  592.6 5.6 collective-permute-start.9
  599.1 195.9 %while.60 = (s32[]{:T(128)}, f32[12,64]{1,0:T(8,128)S(1)}, f32[64]{0:T(128)S(1)}, f32[64,64]{1,0:T(8,128)S(1)}, f32[64]{0:T(128)S(1)}, /*index=5*/f32[64,2]{0,1:...) while((s32[]{:T(128)}, f32[12,64]{1,0:T(8,128)S(1)}, ...), condition=%wide.region_11.12_spmd, body=%wide.region_7.11_spmd.sunk | while | flops 30744452 | bytes 2216265 | solution.py:130
  795.1 105.4 %all-reduce = (f32[12,64]{1,0:T(8,128)S(1)}, f32[64]{0:T(128)S(1)}, f32[64,64]{1,0:T(8,128)S(1)}, f32[64]{0:T(128)S(1)}, f32[64,2]{0,1:T(2,128)S(1)}, /*index=5*/f32[2]{0:T(128)S(1)}) all-reduce(f32[12,64]{1,0:T(8,128)S(1)} %get-tuple-element.299, f32[64]{0:T(128)S(1)} %get-tuple-element.300, ...), channel_id=1, replica_groups=mesh['grp'=16,'col'=32] {'grp','col'}, use_global_device_ids=true, to_apply=%region_12.13 | all-reduce | flops 5122 | bytes 40976 | tf_op jit(solution)/shard_map/psum | solution.py:206
  903.6 5.0 collective-permute-start.11
  908.5 1.9 collective-permute-start.10
  911.0 9.3 collective-permute-done.11
  920.2 6.3 collective-permute-done.10
  (3328 shorter events, 556.3 us)
Async XLA Ops:
  0.6 7.8 copy-start.7
  0.6 7.8 copy-start.8
  1.9 148.4 %collective-permute-start.4 = (f32[2,32,1,128]{3,2,1,0:T(1,128)S(1)}, f32[2,32,1,128]{3,2,1,0:T(1,128)S(1)}, u32[]{:S(2)}, u32[]{:S(2)}) collective-permute-start(f32[2,32,1,128]{3,2,1,0:T(1,128)S(1)} %get-tuple-element.537), channel_id=1, source_target_pairs={{32,0},{64,32},{96,64},{128,96},{160,128},{192,160},{224,192},{256... | collective-permute-start | bytes 98312 | tf_op jit(solution)/shard_map/ppermute | solution.py:19
  3.2 147.1 %collective-permute-start.5 = (f32[2,32,1,128]{3,2,1,0:T(1,128)S(1)}, f32[2,32,1,128]{3,2,1,0:T(1,128)S(1)}, u32[]{:S(2)}, u32[]{:S(2)}) collective-permute-start(f32[2,32,1,128]{3,2,1,0:T(1,128)S(1)} %get-tuple-element.536), channel_id=1, source_target_pairs={{0,32},{32,64},{64,96},{96,128},{128,160},{160,192},{192,224},{224... | collective-permute-start | bytes 98312 | tf_op jit(solution)/shard_map/ppermute | solution.py:16
  14.0 144.9 %collective-permute-start = (f32[2,32,1,128]{3,2,1,0:T(1,128)S(1)}, f32[2,32,1,128]{3,2,1,0:T(1,128)S(1)}, u32[]{:S(2)}, u32[]{:S(2)}) collective-permute-start(f32[2,32,1,128]{3,2,1,0:T(1,128)S(1)} %get-tuple-element.533), channel_id=1, source_target_pairs={{32,0},{64,32},{96,64},{128,96},{160,128},{192,160},{224,192},{256... | collective-permute-start | bytes 98312 | tf_op jit(solution)/shard_map/ppermute | solution.py:19
  15.3 143.6 %collective-permute-start.1 = (f32[2,32,1,128]{3,2,1,0:T(1,128)S(1)}, f32[2,32,1,128]{3,2,1,0:T(1,128)S(1)}, u32[]{:S(2)}, u32[]{:S(2)}) collective-permute-start(f32[2,32,1,128]{3,2,1,0:T(1,128)S(1)} %get-tuple-element.532), channel_id=1, source_target_pairs={{0,32},{32,64},{64,96},{96,128},{128,160},{160,192},{192,224},{224... | collective-permute-start | bytes 98312 | tf_op jit(solution)/shard_map/ppermute | solution.py:16
  150.6 20.1 %collective-permute-start.7 = (f32[2,32,10,1]{3,2,1,0:T(8,128)S(1)}, f32[2,32,10,1]{3,2,1,0:T(8,128)S(1)}, u32[]{:S(2)}, u32[]{:S(2)}) collective-permute-start(f32[2,32,10,1]{3,2,1,0:T(8,128)S(1)} %get-tuple-element.523), channel_id=1, source_target_pairs={{0,1},{1,2},{2,3},{3,4},{4,5},{5,6},{6,7},{7,8},{8,9},{9,10},{10,1... | collective-permute-start | bytes 7688 | tf_op jit(solution)/shard_map/ppermute | solution.py:16
  157.0 15.6 %collective-permute-start.6 = (f32[2,32,10,1]{3,2,1,0:T(8,128)S(1)}, f32[2,32,10,1]{3,2,1,0:T(8,128)S(1)}, u32[]{:S(2)}, u32[]{:S(2)}) collective-permute-start(f32[2,32,10,1]{3,2,1,0:T(8,128)S(1)} %get-tuple-element.522), channel_id=1, source_target_pairs={{1,0},{2,1},{3,2},{4,3},{5,4},{6,5},{7,6},{8,7},{9,8},{10,9},{11,1... | collective-permute-start | bytes 7688 | tf_op jit(solution)/shard_map/ppermute | solution.py:19
  160.7 429.4 %collective-permute-start.3 = (f32[2,32,10,1]{3,2,1,0:T(8,128)}, f32[2,32,10,1]{3,2,1,0:T(8,128)S(1)}, u32[]{:S(2)}, u32[]{:S(2)}) collective-permute-start(f32[2,32,10,1]{3,2,1,0:T(8,128)} %get-tuple-element.521), channel_id=1, source_target_pairs={{0,1},{1,2},{2,3},{3,4},{4,5},{5,6},{6,7},{7,8},{8,9},{9,10},{10,1... | collective-permute-start | bytes 7688 | tf_op jit(solution)/shard_map/ppermute | solution.py:16
  166.5 423.7 %collective-permute-start.2 = (f32[2,32,10,1]{3,2,1,0:T(8,128)}, f32[2,32,10,1]{3,2,1,0:T(8,128)S(1)}, u32[]{:S(2)}, u32[]{:S(2)}) collective-permute-start(f32[2,32,10,1]{3,2,1,0:T(8,128)} %get-tuple-element.520), channel_id=1, source_target_pairs={{1,0},{2,1},{3,2},{4,3},{5,4},{6,5},{7,6},{8,7},{9,8},{10,9},{11,1... | collective-permute-start | bytes 7688 | tf_op jit(solution)/shard_map/ppermute | solution.py:19
  173.7 6.3 copy-start.40
  186.8 6.3 copy-start.40
  199.8 6.3 copy-start.40
  212.8 6.3 copy-start.40
  225.7 6.3 copy-start.40
  238.7 6.3 copy-start.40
  251.7 6.3 copy-start.40
  277.7 6.3 copy-start.40
  290.7 6.3 copy-start.40
  342.7 6.3 copy-start.40
  355.7 6.3 copy-start.40
  407.7 6.3 copy-start.40
  420.6 6.3 copy-start.40
  472.6 6.3 copy-start.40
  524.6 6.3 copy-start.40
  537.6 6.3 copy-start.40
  563.6 6.3 copy-start.40
  576.6 6.3 copy-start.40
  591.3 311.9 %collective-permute-start.8 = (f32[2,32,1,128]{3,2,1,0:T(1,128)S(1)}, f32[2,32,1,128]{3,2,1,0:T(1,128)S(1)}, u32[]{:S(2)}, u32[]{:S(2)}) collective-permute-start(f32[2,32,1,128]{3,2,1,0:T(1,128)S(1)} %get-tuple-element.531), channel_id=1, source_target_pairs={{32,0},{64,32},{96,64},{128,96},{160,128},{192,160},{224,192},{256... | collective-permute-start | bytes 98312 | tf_op jit(solution)/shard_map/ppermute | solution.py:19
  592.6 310.6 %collective-permute-start.9 = (f32[2,32,1,128]{3,2,1,0:T(1,128)S(1)}, f32[2,32,1,128]{3,2,1,0:T(1,128)S(1)}, u32[]{:S(2)}, u32[]{:S(2)}) collective-permute-start(f32[2,32,1,128]{3,2,1,0:T(1,128)S(1)} %get-tuple-element.530), channel_id=1, source_target_pairs={{0,32},{32,64},{64,96},{96,128},{128,160},{160,192},{192,224},{224... | collective-permute-start | bytes 98312 | tf_op jit(solution)/shard_map/ppermute | solution.py:16
  903.6 16.7 %collective-permute-start.11 = (f32[2,32,10,1]{3,2,1,0:T(8,128)S(1)}, f32[2,32,10,1]{3,2,1,0:T(8,128)S(1)}, u32[]{:S(2)}, u32[]{:S(2)}) collective-permute-start(f32[2,32,10,1]{3,2,1,0:T(8,128)S(1)} %get-tuple-element.519), channel_id=1, source_target_pairs={{0,1},{1,2},{2,3},{3,4},{4,5},{5,6},{6,7},{7,8},{8,9},{9,10},{10,1... | collective-permute-start | bytes 7688 | tf_op jit(solution)/shard_map/ppermute | solution.py:16
  908.5 18.0 %collective-permute-start.10 = (f32[2,32,10,1]{3,2,1,0:T(8,128)S(1)}, f32[2,32,10,1]{3,2,1,0:T(8,128)S(1)}, u32[]{:S(2)}, u32[]{:S(2)}) collective-permute-start(f32[2,32,10,1]{3,2,1,0:T(8,128)S(1)} %get-tuple-element.518), channel_id=1, source_target_pairs={{1,0},{2,1},{3,2},{4,3},{5,4},{6,5},{7,6},{8,7},{9,8},{10,9},{11,1... | collective-permute-start | bytes 7688 | tf_op jit(solution)/shard_map/ppermute | solution.py:19
  (679 other events, 870.9 us)
where the time goes:
time: 941 us; the launch traced here: 928 us
  local copies, waits for them, and re-layouts  316 us (34%)
  matrix products  209 us (22%)
  loops' own time  189 us (20%)
  blocking collectives  105 us (11%)
  other arithmetic  46.2 us (5%)
  starting transfers between devices  41 us (4%)
  waiting for transfers between devices  19.7 us (2%)
    while x1920, local copies, waits for them, and re-layouts  250 us
    another operation x2, loops' own time, backward_lines(): lax.scan(backward_one_line, running, jnp.arange(solid.shape[0], dtype=jnp...  125 us
    psum x1, blocking collectives, shards(): lax.psum((running[0], running[1], running[2], running[3], running[4], run...  105 us
    another operation x1, loops' own time, forward_coupling(): lax.map(forward_one_line, jnp.arange(solid.shape[0], dtype=jnp.int32))  64.3 us
    dynamic_slice x96, local copies, waits for them, and re-layouts, forward_coupling(): lax.map(forward_one_line, jnp.arange(solid.shape[0], dtype=jnp.int32))  55.9 us
    dot_general x64, matrix products, backprop(): jnp.dot(w_out, d_logits, preferred_element_type=jnp.float32)  39.4 us
    dot_general x64, matrix products, network(): jnp.dot(w_in.T, features, preferred_element_type=jnp.float32)  35.9 us
    dot_general x64, matrix products, backprop(): jnp.dot(w_mid, d_hidden_two, preferred_element_type=jnp.float32)  33.9 us
  transfers between devices with their start and end apart: 12, of which 4 were waited for; matrix products, arithmetic and copies ran while one was open for 44% of the time, Pallas kernels for 0%

commit v1 on v0

--- a/solution.py
+++ b/solution.py
@@ -203,9 +203,9 @@
         + jnp.stack([swing_term, -swing_term])
         + d_features
     )
-    summed = lax.psum(
-        (running[0], running[1], running[2], running[3], running[4], running[5]), ("grp", "col")
-    )
+    x0 = (running[0], running[1], running[2], running[3], running[4], running[5])
+    block_now = jax.lax.psum(x0, "col")
+    summed = jax.lax.psum(block_now, "grp")
     cell_count = solid_temp.size * lax.axis_size("grp") * lax.axis_size("col")
     scale = loss_gain / math.sqrt(cell_count)
     return (

time: 941 us -> 1030 us (1.095)
  the two profiles are of different devices: /device:TPU:19 before, /device:TPU:1 now
where the time goes in v1:
time: 1030 us; the launch traced here: 1020 us
  local copies, waits for them, and re-layouts  313 us (30%)
  matrix products  209 us (20%)
  loops' own time  189 us (18%)
  blocking collectives  188 us (18%)
  starting transfers between devices  55.7 us (5%)
  other arithmetic  46.3 us (4%)
  waiting for transfers between devices  16.2 us (2%)
    while x1920, local copies, waits for them, and re-layouts  247 us
    psum x1, blocking collectives, shards(): block_now = jax.lax.psum(x0, 'col')  133 us
    another operation x2, loops' own time, backward_lines(): lax.scan(backward_one_line, running, jnp.arange(solid.shape[0], dtype=jnp...  124 us
    another operation x1, loops' own time, forward_coupling(): lax.map(forward_one_line, jnp.arange(solid.shape[0], dtype=jnp.int32))  64.3 us
    dynamic_slice x96, local copies, waits for them, and re-layouts, forward_coupling(): lax.map(forward_one_line, jnp.arange(solid.shape[0], dtype=jnp.int32))  56 us
    psum x1, blocking collectives, shards(): summed = jax.lax.psum(block_now, 'grp')  55.3 us
    ppermute x6, starting transfers between devices, padded_2(): lax.ppermute(lax.slice_in_dim(block, block.shape[dim] - width, None, axis...  39.8 us
    dot_general x64, matrix products, backprop(): jnp.dot(w_out, d_logits, preferred_element_type=jnp.float32)  39.7 us
  transfers between devices with their start and end apart: 12, of which 2 were waited for; matrix products, arithmetic and copies ran while one was open for 40% of the time, Pallas kernels for 0%

profile of v1, /device:TPU:1, one launch (start us, length us, event | category | flops | bytes accessed | tf_op | source)
XLA Modules:
  0.0 1018.6 jit_solution(4187620168065603818)
XLA Ops:
  0.7 1.2 fusion.89
  1.9 1.3 collective-permute-start.4
  3.2 4.6 collective-permute-start.5
  9.1 2.7 add_bitcast_fusion.1
  11.8 2.7 add_bitcast_fusion
  14.7 1.3 collective-permute-start
  16.0 4.9 collective-permute-start.1
  21.7 128.7 %while.59 = (s32[]{:T(128)}, f32[32,8,128]{2,1,0:T(8,128)S(1)}, s32[32]{0:T(128)S(1)}, bf16[10,32,8,128]{3,2,1,0:T(8,128)(2,1)}, bf16[32,8,128]{2,1,0:T(8,128)(2...) while((s32[]{:T(128)}, f32[32,8,128]{2,1,0:T(8,128)S(1)}, ...), condition=%wide.region_1.2_spmd, body=%wide.region_0.1_spmd.sunk | while | flops 10574853 | bytes 510433 | solution.py:110
  151.4 5.6 collective-permute-start.7
  157.1 4.0 collective-permute-start.6
  161.7 1.2 fusion.96
  162.9 2.4 collective-permute-start.3
  165.3 1.9 collective-permute-start.2
  167.3 7.1 collective-permute-done.6
  175.6 413.0 %while.61 = (s32[]{:T(128)}, f32[12,64]{1,0:T(8,128)S(1)}, f32[64]{0:T(128)}, f32[64,64]{1,0:T(8,128)S(1)}, f32[64]{0:T(128)}, /*index=5*/f32[64,2]{0,1:T(2,128)...) while((s32[]{:T(128)}, f32[12,64]{1,0:T(8,128)S(1)}, ...), condition=%wide.region_6.7_spmd.clone, body=%wide.region_2.6_spmd.clone.sunk | while | flops 30749576 | bytes 3280900 | solution.py:130
  181.8 0.9 convert_reduce_fusion.16
  220.5 0.9 convert_reduce_fusion.16
  259.2 0.9 convert_reduce_fusion.16
  297.9 0.9 convert_reduce_fusion.16
  336.6 0.9 convert_reduce_fusion.16
  375.4 0.9 convert_reduce_fusion.16
  452.8 0.9 convert_reduce_fusion.16
  491.5 0.9 convert_reduce_fusion.16
  530.2 0.9 convert_reduce_fusion.16
  590.3 1.3 collective-permute-start.8
  591.6 4.0 collective-permute-start.9
  596.4 195.9 %while.60 = (s32[]{:T(128)}, f32[12,64]{1,0:T(8,128)S(1)}, f32[64]{0:T(128)S(1)}, f32[64,64]{1,0:T(8,128)S(1)}, f32[64]{0:T(128)S(1)}, /*index=5*/f32[64,2]{0,1:...) while((s32[]{:T(128)}, f32[12,64]{1,0:T(8,128)S(1)}, ...), condition=%wide.region_11.12_spmd, body=%wide.region_7.11_spmd.sunk | while | flops 30744452 | bytes 2216265 | solution.py:130
  792.4 132.7 %all-reduce = (f32[12,64]{1,0:T(8,128)S(1)}, f32[64]{0:T(128)S(1)}, f32[64,64]{1,0:T(8,128)S(1)}, f32[64]{0:T(128)S(1)}, f32[64,2]{0,1:T(2,128)S(1)}, /*index=5*/f32[2]{0:T(128)S(1)}) all-reduce(f32[12,64]{1,0:T(8,128)S(1)} %get-tuple-element.299, f32[64]{0:T(128)S(1)} %get-tuple-element.300, ...), channel_id=1, replica_groups=mesh['grp'=16,'col'=32] {'col'}, use_global_device_ids=true, to_apply=%region_12.13 | all-reduce | flops 5122 | bytes 40976 | tf_op jit(solution)/shard_map/psum | solution.py:207
  925.1 55.3 %all-reduce.1 = (f32[12,64]{1,0:T(8,128)S(1)}, f32[64]{0:T(128)S(1)}, f32[64,64]{1,0:T(8,128)S(1)}, f32[64]{0:T(128)S(1)}, f32[64,2]{0,1:T(2,128)S(1)}, /*index=5*/f32[2]{0:T(128)S(1)}) all-reduce(f32[12,64]{1,0:T(8,128)S(1)} %get-tuple-element.472, f32[64]{0:T(128)S(1)} %get-tuple-element.473, ...), channel_id=1, replica_groups=mesh['grp'=16,'col'=32] {'grp'}, use_global_device_ids=true, to_apply=%region_13.14 | all-reduce | flops 5122 | bytes 40976 | tf_op jit(solution)/shard_map/psum | solution.py:208
  983.5 18.3 %collective-permute-start.11 = (f32[2,32,10,1]{3,2,1,0:T(8,128)S(1)}, f32[2,32,10,1]{3,2,1,0:T(8,128)S(1)}, u32[]{:S(2)}, u32[]{:S(2)}) collective-permute-start(f32[2,32,10,1]{3,2,1,0:T(8,128)S(1)} %get-tuple-element.525), channel_id=1, source_target_pairs={{0,1},{1,2},{2,3},{3,4},{4,5},{5,6},{6,7},{7,8},{8,9},{9,10},{10,1... | collective-permute-start | bytes 7688 | tf_op jit(solution)/shard_map/ppermute | solution.py:16
  1001.8 6.1 collective-permute-start.10
  1008.4 9.1 collective-permute-done.10
  (3329 shorter events, 552.9 us)
Async XLA Ops:
  0.6 8.4 copy-start.7
  0.6 8.4 copy-start.8
  1.9 149.3 %collective-permute-start.4 = (f32[2,32,1,128]{3,2,1,0:T(1,128)S(1)}, f32[2,32,1,128]{3,2,1,0:T(1,128)S(1)}, u32[]{:S(2)}, u32[]{:S(2)}) collective-permute-start(f32[2,32,1,128]{3,2,1,0:T(1,128)S(1)} %get-tuple-element.543), channel_id=1, source_target_pairs={{32,0},{64,32},{96,64},{128,96},{160,128},{192,160},{224,192},{256... | collective-permute-start | bytes 98312 | tf_op jit(solution)/shard_map/ppermute | solution.py:19
  3.2 148.0 %collective-permute-start.5 = (f32[2,32,1,128]{3,2,1,0:T(1,128)S(1)}, f32[2,32,1,128]{3,2,1,0:T(1,128)S(1)}, u32[]{:S(2)}, u32[]{:S(2)}) collective-permute-start(f32[2,32,1,128]{3,2,1,0:T(1,128)S(1)} %get-tuple-element.542), channel_id=1, source_target_pairs={{0,32},{32,64},{64,96},{96,128},{128,160},{160,192},{192,224},{224... | collective-permute-start | bytes 98312 | tf_op jit(solution)/shard_map/ppermute | solution.py:16
  14.5 6.3 copy-start.1
  14.6 6.3 copy-start
  14.7 146.4 %collective-permute-start = (f32[2,32,1,128]{3,2,1,0:T(1,128)S(1)}, f32[2,32,1,128]{3,2,1,0:T(1,128)S(1)}, u32[]{:S(2)}, u32[]{:S(2)}) collective-permute-start(f32[2,32,1,128]{3,2,1,0:T(1,128)S(1)} %get-tuple-element.539), channel_id=1, source_target_pairs={{32,0},{64,32},{96,64},{128,96},{160,128},{192,160},{224,192},{256... | collective-permute-start | bytes 98312 | tf_op jit(solution)/shard_map/ppermute | solution.py:19
  16.0 145.1 %collective-permute-start.1 = (f32[2,32,1,128]{3,2,1,0:T(1,128)S(1)}, f32[2,32,1,128]{3,2,1,0:T(1,128)S(1)}, u32[]{:S(2)}, u32[]{:S(2)}) collective-permute-start(f32[2,32,1,128]{3,2,1,0:T(1,128)S(1)} %get-tuple-element.538), channel_id=1, source_target_pairs={{0,32},{32,64},{64,96},{96,128},{128,160},{160,192},{192,224},{224... | collective-permute-start | bytes 98312 | tf_op jit(solution)/shard_map/ppermute | solution.py:16
  151.4 15.8 %collective-permute-start.7 = (f32[2,32,10,1]{3,2,1,0:T(8,128)S(1)}, f32[2,32,10,1]{3,2,1,0:T(8,128)S(1)}, u32[]{:S(2)}, u32[]{:S(2)}) collective-permute-start(f32[2,32,10,1]{3,2,1,0:T(8,128)S(1)} %get-tuple-element.529), channel_id=1, source_target_pairs={{0,1},{1,2},{2,3},{3,4},{4,5},{5,6},{6,7},{7,8},{8,9},{9,10},{10,1... | collective-permute-start | bytes 7688 | tf_op jit(solution)/shard_map/ppermute | solution.py:16
  157.1 17.3 %collective-permute-start.6 = (f32[2,32,10,1]{3,2,1,0:T(8,128)S(1)}, f32[2,32,10,1]{3,2,1,0:T(8,128)S(1)}, u32[]{:S(2)}, u32[]{:S(2)}) collective-permute-start(f32[2,32,10,1]{3,2,1,0:T(8,128)S(1)} %get-tuple-element.528), channel_id=1, source_target_pairs={{1,0},{2,1},{3,2},{4,3},{5,4},{6,5},{7,6},{8,7},{9,8},{10,9},{11,1... | collective-permute-start | bytes 7688 | tf_op jit(solution)/shard_map/ppermute | solution.py:19
  162.9 426.2 %collective-permute-start.3 = (f32[2,32,10,1]{3,2,1,0:T(8,128)}, f32[2,32,10,1]{3,2,1,0:T(8,128)S(1)}, u32[]{:S(2)}, u32[]{:S(2)}) collective-permute-start(f32[2,32,10,1]{3,2,1,0:T(8,128)} %get-tuple-element.527), channel_id=1, source_target_pairs={{0,1},{1,2},{2,3},{3,4},{4,5},{5,6},{6,7},{7,8},{8,9},{9,10},{10,1... | collective-permute-start | bytes 7688 | tf_op jit(solution)/shard_map/ppermute | solution.py:16
  165.3 423.7 %collective-permute-start.2 = (f32[2,32,10,1]{3,2,1,0:T(8,128)}, f32[2,32,10,1]{3,2,1,0:T(8,128)S(1)}, u32[]{:S(2)}, u32[]{:S(2)}) collective-permute-start(f32[2,32,10,1]{3,2,1,0:T(8,128)} %get-tuple-element.526), channel_id=1, source_target_pairs={{1,0},{2,1},{3,2},{4,3},{5,4},{6,5},{7,6},{8,7},{9,8},{10,9},{11,1... | collective-permute-start | bytes 7688 | tf_op jit(solution)/shard_map/ppermute | solution.py:19
  175.6 6.2 copy-start.40
  201.4 6.2 copy-start.40
  214.3 6.2 copy-start.40
  227.2 6.2 copy-start.40
  240.1 6.2 copy-start.40
  253.0 6.2 copy-start.40
  265.9 6.2 copy-start.40
  278.8 6.2 copy-start.40
  291.7 6.2 copy-start.40
  304.6 6.2 copy-start.40
  317.5 6.2 copy-start.40
  330.4 6.2 copy-start.40
  343.3 6.2 copy-start.40
  524.0 6.2 copy-start.40
  562.7 6.2 copy-start.40
  575.6 6.2 copy-start.40
  590.3 392.9 %collective-permute-start.8 = (f32[2,32,1,128]{3,2,1,0:T(1,128)S(1)}, f32[2,32,1,128]{3,2,1,0:T(1,128)S(1)}, u32[]{:S(2)}, u32[]{:S(2)}) collective-permute-start(f32[2,32,1,128]{3,2,1,0:T(1,128)S(1)} %get-tuple-element.537), channel_id=1, source_target_pairs={{32,0},{64,32},{96,64},{128,96},{160,128},{192,160},{224,192},{256... | collective-permute-start | bytes 98312 | tf_op jit(solution)/shard_map/ppermute | solution.py:19
  591.6 391.6 %collective-permute-start.9 = (f32[2,32,1,128]{3,2,1,0:T(1,128)S(1)}, f32[2,32,1,128]{3,2,1,0:T(1,128)S(1)}, u32[]{:S(2)}, u32[]{:S(2)}) collective-permute-start(f32[2,32,1,128]{3,2,1,0:T(1,128)S(1)} %get-tuple-element.536), channel_id=1, source_target_pairs={{0,32},{32,64},{64,96},{96,128},{128,160},{160,192},{192,224},{224... | collective-permute-start | bytes 98312 | tf_op jit(solution)/shard_map/ppermute | solution.py:16
  983.5 24.9 %collective-permute-start.11 = (f32[2,32,10,1]{3,2,1,0:T(8,128)S(1)}, f32[2,32,10,1]{3,2,1,0:T(8,128)S(1)}, u32[]{:S(2)}, u32[]{:S(2)}) collective-permute-start(f32[2,32,10,1]{3,2,1,0:T(8,128)S(1)} %get-tuple-element.525), channel_id=1, source_target_pairs={{0,1},{1,2},{2,3},{3,4},{4,5},{5,6},{6,7},{7,8},{8,9},{9,10},{10,1... | collective-permute-start | bytes 7688 | tf_op jit(solution)/shard_map/ppermute | solution.py:16
  1001.8 15.7 %collective-permute-start.10 = (f32[2,32,10,1]{3,2,1,0:T(8,128)S(1)}, f32[2,32,10,1]{3,2,1,0:T(8,128)S(1)}, u32[]{:S(2)}, u32[]{:S(2)}) collective-permute-start(f32[2,32,10,1]{3,2,1,0:T(8,128)S(1)} %get-tuple-element.524), channel_id=1, source_target_pairs={{1,0},{2,1},{3,2},{4,3},{5,4},{6,5},{7,6},{8,7},{9,8},{10,9},{11,1... | collective-permute-start | bytes 7688 | tf_op jit(solution)/shard_map/ppermute | solution.py:19
  (679 other events, 859.5 us)
